TPU v7x, 512 devices: a whole 4x4x16 slice. The times are simulated.
512 devices in a mesh: slab: 64 (over z_lo, x, core), grp: 8 (over z_hi, y).
Axes of the slice: x: 4, y: 4, z: 16 (z_hi: 2, z_lo: 8; z = z_hi * 8 + z_lo), core: 2. Of those that a mesh axis runs over, the one named last changes fastest.
Arguments:
- adj_out: float32 [5, 512, 256, 256], P(None, 'grp', 'slab'), may hold values from -6 to 6
- advect: bfloat16 [3, 512, 256, 256], P(None, 'grp', 'slab'), may hold values from -4 to 4
- viscosity: bfloat16 [512, 256, 256], P('grp', 'slab'), may hold values from 0.099609375 to 0.796875
- body_mask: int32 [512, 256, 256], P('grp', 'slab'), may hold values 0 or 1
- marker_x: int32 [2048], replicated, may hold values from 128 to 191
- marker_z: int32 [2048], replicated, may hold values from 0 to 255
- marker_y: int32 [2048], replicated, may hold values from 64 to 191
- drag_weight: float32 [2048], replicated, may hold values from -5 to 5
- inv_x: float32 [512, 512], P(None, 'grp'), may hold values from 0 to 1, as said below
- inv_y: float32 [256, 256], replicated, may hold values from 0 to 1, as said below
- inv_z: float32 [256, 256], replicated, may hold values from 0 to 1, as said below
Outputs:
- state_adjoint: float32 [5, 512, 256, 256], P(None, 'grp', 'slab')
Inputs may be any that keep to these rules, and one draw needn't show every extreme that they name: `inv_x`: entries of a given inverse. `inv_y`: entries of a given inverse. `inv_z`: entries of a given inverse.
All inputs are finite; a program needn't handle non-finite values. No bound on the sum of `body_mask` on one device may be relied on, other than what follows from the above.
Results may differ from a plain program's by a relative error of at most 0.0003.
Values sent between devices are 32-bit elements; how exact they have to be, the bound alone decides.
No kernel may reach another device: no remote copies, remote signals or barrier semaphores. Data moves between devices by JAX's collectives and lax.ppermute only.
A program may use at most 64 MiB of HBM per device.

v0:
```python
import jax
import jax.numpy as jnp
from jax import lax
from jax.sharding import PartitionSpec as P

time_step = 0.08
highest = lax.Precision.HIGHEST


def extended(cells, sides, width):
    for axis, dim in sides:
        count = lax.axis_size(axis)
        ends = count - 1
        head = lax.slice_in_dim(cells, 0, width, axis=dim)
        tail = lax.slice_in_dim(cells, cells.shape[dim] - width, cells.shape[dim], axis=dim)
        cells = jnp.concatenate(
            [
                lax.ppermute(tail, axis, [(i, (i + 1) % count) for i in range(ends)]),
                cells,
                lax.ppermute(head, axis, [((i + 1) % count, i) for i in range(ends)]),
            ],
            axis=dim,
        )
    return cells


def body(
    adj_out,
    advect,
    viscosity,
    body_mask,
    marker_x,
    marker_z,
    marker_y,
    drag_weight,
    inv_x,
    inv_y,
    inv_z,
):
    fields, x_rows, z_rows, y_cells = adj_out.shape
    x_offset = lax.axis_index("grp") * x_rows
    z_offset = lax.axis_index("slab") * z_rows
    local_x = marker_x - x_offset
    local_z = marker_z - z_offset
    inside = (local_x >= 0) & (local_x < x_rows) & (local_z >= 0) & (local_z < z_rows)
    flat_index = jnp.where(inside, (local_x * z_rows + local_z) * y_cells + marker_y, 0)
    pushed = jax.ops.segment_sum(
        jnp.where(inside, drag_weight, 0.0), flat_index, num_segments=x_rows * z_rows * y_cells
    )
    seeded = adj_out.at[0].add(pushed.reshape(x_rows, z_rows, y_cells))
    zlines = lax.all_to_all(seeded, "slab", split_axis=1, concat_axis=2, tiled=True)
    zlines = jnp.einsum("jk,cxjy->cxky", inv_z, zlines, precision=highest)
    zlines = jnp.einsum("jk,cxzj->cxzk", inv_y, zlines, precision=highest)
    returned = lax.all_to_all(zlines, "slab", split_axis=2, concat_axis=1, tiled=True)
    solved = jnp.einsum(
        "jk,cjzy->ckzy",
        inv_x,
        lax.all_gather(returned, "grp", axis=1, tiled=True),
        precision=highest,
    )
    masked = solved * body_mask.astype(jnp.float32)
    rimmed = extended(masked, (("slab", 2), ("grp", 1)), 1)
    centre = rimmed[:, 1:-1, 1:-1, :]
    y_padded = jnp.pad(centre, ((0, 0), (0, 0), (0, 0), (1, 1)))
    grad_x = (rimmed[:, 2:, 1:-1, :] - rimmed[:, :-2, 1:-1, :]) * 0.5
    grad_z = (rimmed[:, 1:-1, 2:, :] - rimmed[:, 1:-1, :-2, :]) * 0.5
    grad_y = (y_padded[..., 2:] - y_padded[..., :-2]) * 0.5
    laplace = (
        rimmed[:, 2:, 1:-1, :]
        + rimmed[:, :-2, 1:-1, :]
        + rimmed[:, 1:-1, 2:, :]
        + rimmed[:, 1:-1, :-2, :]
        + y_padded[..., 2:]
        + y_padded[..., :-2]
        - 6.0 * centre
    )
    velocity = advect.astype(jnp.float32)
    viscous = viscosity.astype(jnp.float32)
    change = velocity[0] * grad_x + velocity[1] * grad_z + velocity[2] * grad_y + viscous * laplace
    return centre + time_step * change


def solution(mesh):
    in_specs = (
        P(None, "grp", "slab", None),
        P(None, "grp", "slab", None),
        P("grp", "slab", None),
        P("grp", "slab", None),
        P(),
        P(),
        P(),
        P(),
        P(None, "grp"),
        P(),
        P(),
    )
    out_specs = P(None, "grp", "slab", None)
    return jax.shard_map(body, mesh=mesh, in_specs=in_specs, out_specs=out_specs, check_vma=False)
```

profile of v0, /device:TPU:352, one launch (start us, length us, event | category | flops | bytes accessed | tf_op | source)
XLA Modules:
  0.0 591.5 jit_solution(2021794597790402186)
XLA Ops:
  6.5 0.8 add_select_fusion
  7.3 0.7 broadcast_select_fusion
  8.1 14.8 %scatter_custom_fusion = f32[65536]{0:T(1024)S(1)} fusion(s32[2048]{0:T(1024)S(1)} %add_select_fusion, f32[2048]{0:T(1024)S(1)} %broadcast_select_fusion, f32[]{:T(128)} %constant.45.clone.1), kind=kCustom, calls=%fused_computation.27 | custom fusion | flops 2048 | bytes 262148 | tf_op jit(solution)/shard_map/scatter-add | solution.py:47
  22.8 0.1 reshape.62
  23.0 1.5 copy.57
  24.5 0.1 fusion.4
  24.6 68.9 %all_to_all.21 = f32[5,64,4,256]{3,2,0,1:T(4,128)S(1)} all-to-all(f32[5,64,4,256]{3,2,0,1:T(4,128)S(1)} %fusion.4), channel_id=1, replica_groups=mesh['slab'=64,'grp'=8] {'slab'}, dimensions={1} | all-to-all | bytes 2621440 | tf_op jit(solution)/shard_map/all_to_all | solution.py:51
  93.5 0.2 copy.58
  93.8 0.5 reshape.63
  94.3 2.2 convolution_bitcast_fusion.1
  96.5 2.3 convolution_bitcast_fusion
  98.8 1.3 copy.61
  100.1 70.3 %all_to_all.22 = f32[5,1,256,256]{3,1,0,2:T(1,128)S(1)} all-to-all(f32[5,1,256,256]{3,1,0,2:T(1,128)S(1)} %copy.61), channel_id=1, replica_groups=mesh['slab'=64,'grp'=8] {'slab'}, dimensions={2} | all-to-all | bytes 2621440 | tf_op jit(solution)/shard_map/all_to_all | solution.py:54
  170.4 0.3 copy.75
  170.7 1.8 copy.63
  172.5 0.9 copy-done.2
  173.5 0.1 copy.64
  173.6 324.0 %all-gather.2.cloned.1.call-done = f32[5,512,4,256]{3,1,2,0:T(8,128)} async-done(((f32[5,64,4,256]{3,1,2,0:T(8,128)}), f32[5,512,4,256]{3,1,2,0:T(8,128)}) %all-gather.2.cloned.1.call-update) | async-done | bytes 10485776 | tf_op jit(solution)/shard_map/all_gather | solution.py:58
  497.6 9.5 %fusion = f32[5,64,4,256]{3,1,2,0:T(8,128)S(1)} fusion(f32[5,512,4,256]{3,1,2,0:T(8,128)} %all-gather.2.cloned.1.call-done, f32[64,4,256]{2,0,1:T(8,128)S(1)} %copy.64, f32[512,64]{0,1:T(8,128)S(1)} %copy-done.4), kind=kOutput, calls=%fused_computation.6 | convolution fusion | flops 2013593600 | bytes 12189696 | tf_op jit(solution)/shard_map/jk,cjzy->ckzy/dot_general | solution.py:55
  507.2 0.1 fusion.10
  507.2 2.1 collective-permute-start
  509.3 38.0 %collective-permute-start.1 = (f32[5,64,1,256]{3,1,2,0:T(8,128)S(1)}, f32[5,64,1,256]{3,1,2,0:T(8,128)S(1)}, u32[]{:S(2)}, u32[]{:S(2)}) collective-permute-start(f32[5,64,1,256]{3,1,2,0:T(8,128)S(1)} %get-tuple-element.20), channel_id=1, source_target_pairs={{8,0},{16,8},{24,16},{32,24},{40,32},{48,40},{56,48},{64,56},{72,6... | collective-permute-start | bytes 983048 | tf_op jit(solution)/shard_map/ppermute | solution.py:20
  547.3 0.1 convert_element_type.12
  547.5 2.7 collective-permute-done
  550.1 2.1 collective-permute-done.1
  552.3 11.7 %collective-permute-start.2 = (f32[5,1,6,256]{3,1,2,0:T(1,128)S(1)}, f32[5,1,6,256]{3,1,2,0:T(1,128)S(1)}, u32[]{:S(2)}, u32[]{:S(2)}) collective-permute-start(f32[5,1,6,256]{3,1,2,0:T(1,128)S(1)} %get-tuple-element.18), channel_id=1, source_target_pairs={{1,0},{2,1},{3,2},{4,3},{5,4},{6,5},{7,6},{9,8},{10,9},{11,10},{12... | collective-permute-start | bytes 92168 | tf_op jit(solution)/shard_map/ppermute | solution.py:20
  564.0 2.1 collective-permute-start.3
  566.1 0.2 fusion.3
  566.3 0.1 copy.65
  566.5 14.3 %collective-permute-done.3 = f32[5,1,6,256]{3,1,2,0:T(1,128)S(1)} collective-permute-done((f32[5,1,6,256]{3,1,2,0:T(1,128)S(1)}, f32[5,1,6,256]{3,1,2,0:T(1,128)S(1)}, u32[]{:S(2)}, u32[]{:S(2)}) %collective-permute-start.3) | collective-permute-done | bytes 30752 | tf_op jit(solution)/shard_map/ppermute | solution.py:18
  580.7 2.0 multiply_add_fusion
  582.8 1.9 copy.69
  (19 shorter events, 0.3 us)
Async XLA Ops:
  6.5 87.7 %copy-start = (f32[256,256]{1,0:T(8,128)S(1)}, f32[256,256]{1,0:T(8,128)}, u32[]{:S(2)}) copy-start(f32[256,256]{1,0:T(8,128)} %param.23) | copy-start | bytes 786436
  6.5 491.1 %all-gather.2.cloned.1.call-start = ((), (), s32[]{:S(2)}) async-start(), calls=%async_computation.2 | async-start | bytes 11796480 | tf_op jit(solution)/shard_map/all_gather | solution.py:58
  94.2 2.2 copy-start.3
  172.5 0.9 copy-start.2
  172.5 325.1 %copy-start.4 = (f32[512,64]{0,1:T(8,128)S(1)}, f32[512,64]{0,1:T(8,128)}, u32[]{:S(2)}) copy-start(f32[512,64]{0,1:T(8,128)} %param.21) | copy-start | bytes 393220
  507.1 40.2 %copy-start.1 = (bf16[3,64,4,256]{3,2,1,0:T(4,128)(2,1)S(1)}, bf16[3,64,4,256]{3,2,1,0:T(4,128)(2,1)}, u32[]{:S(2)}) copy-start(bf16[3,64,4,256]{3,2,1,0:T(4,128)(2,1)} %param.14) | copy-start | bytes 1179652
  507.2 42.9 %collective-permute-start = (f32[5,64,1,256]{3,1,2,0:T(8,128)S(1)}, f32[5,64,1,256]{3,1,2,0:T(8,128)S(1)}, u32[]{:S(2)}, u32[]{:S(2)}) collective-permute-start(f32[5,64,1,256]{3,1,2,0:T(8,128)S(1)} %get-tuple-element.19), channel_id=1, source_target_pairs={{0,8},{8,16},{16,24},{24,32},{32,40},{40,48},{48,56},{56,64},{64,7... | collective-permute-start | bytes 983048 | tf_op jit(solution)/shard_map/ppermute | solution.py:18
  509.3 42.9 %collective-permute-start.1 = (f32[5,64,1,256]{3,1,2,0:T(8,128)S(1)}, f32[5,64,1,256]{3,1,2,0:T(8,128)S(1)}, u32[]{:S(2)}, u32[]{:S(2)}) collective-permute-start(f32[5,64,1,256]{3,1,2,0:T(8,128)S(1)} %get-tuple-element.20), channel_id=1, source_target_pairs={{8,0},{16,8},{24,16},{32,24},{40,32},{48,40},{56,48},{64,56},{72,6... | collective-permute-start | bytes 983048 | tf_op jit(solution)/shard_map/ppermute | solution.py:20
  552.3 14.2 %collective-permute-start.2 = (f32[5,1,6,256]{3,1,2,0:T(1,128)S(1)}, f32[5,1,6,256]{3,1,2,0:T(1,128)S(1)}, u32[]{:S(2)}, u32[]{:S(2)}) collective-permute-start(f32[5,1,6,256]{3,1,2,0:T(1,128)S(1)} %get-tuple-element.18), channel_id=1, source_target_pairs={{1,0},{2,1},{3,2},{4,3},{5,4},{6,5},{7,6},{9,8},{10,9},{11,10},{12... | collective-permute-start | bytes 92168 | tf_op jit(solution)/shard_map/ppermute | solution.py:20
  564.0 2.5 copy-start.5
  564.0 16.7 %collective-permute-start.3 = (f32[5,1,6,256]{3,1,2,0:T(1,128)S(1)}, f32[5,1,6,256]{3,1,2,0:T(1,128)S(1)}, u32[]{:S(2)}, u32[]{:S(2)}) collective-permute-start(f32[5,1,6,256]{3,1,2,0:T(1,128)S(1)} %get-tuple-element.17), channel_id=1, source_target_pairs={{0,1},{1,2},{2,3},{3,4},{4,5},{5,6},{6,7},{8,9},{9,10},{10,11},{11... | collective-permute-start | bytes 92168 | tf_op jit(solution)/shard_map/ppermute | solution.py:18
Sparse Core Ops, SparseCore 0:
  172.7 324.8 all-gather.1
where the time goes:
time: 592 us
  waiting for transfers between devices  343 us (58%)
  blocking collectives  139 us (23%)
  starting transfers between devices  53.8 us (9%)
  other arithmetic  18.8 us (3%)
  matrix products  14 us (2%)
  between operations  13.6 us (2%)
  local copies, waits for them, and re-layouts  8.92 us (2%)
    all_gather x1, waiting for transfers between devices, body(): lax.all_gather(returned, 'grp', axis=1, tiled=True)  324 us
    all_to_all x1, blocking collectives, body(): lax.all_to_all(zlines, 'slab', split_axis=2, concat_axis=1, tiled=True)  70.3 us
    all_to_all x1, blocking collectives, body(): lax.all_to_all(seeded, 'slab', split_axis=1, concat_axis=2, tiled=True)  68.9 us
    ppermute x2, starting transfers between devices, extended(): lax.ppermute(head, axis, [((i + 1) % count, i) for i in range(ends)])  49.7 us
    ppermute x2, waiting for transfers between devices, extended(): lax.ppermute(tail, axis, [(i, (i + 1) % count) for i in range(ends)])  17 us
    scatter-add x1, other arithmetic, body(): jax.ops.segment_sum(jnp.where(inside, drag_weight, 0.0), flat_index, num_...  14.8 us
  transfers between devices with their start and end apart: 5, of which 4 were waited for; matrix products, arithmetic and copies ran while one was open for 0% of the time, Pallas kernels for 0%

commit v1 on v0

--- a/solution.py
+++ b/solution.py
@@ -55,7 +55,9 @@
     solved = jnp.einsum(
         "jk,cjzy->ckzy",
         inv_x,
-        lax.all_gather(returned, "grp", axis=1, tiled=True),
+        jnp.concatenate(
+            lax.all_to_all(jnp.stack([returned] * lax.axis_size("grp")), "grp", 0, 0), axis=1
+        ),
         precision=highest,
     )
     masked = solved * body_mask.astype(jnp.float32)

time: 592 us -> 749 us (1.27)
  the two profiles are of different devices: /device:TPU:352 before, /device:TPU:451 now
where the time goes in v1:
time: 749 us; the launch traced here: 748 us
  waiting for transfers between devices  385 us (51%)
  starting transfers between devices  179 us (24%)
  blocking collectives  136 us (18%)
  other arithmetic  18.8 us (3%)
  local copies, waits for them, and re-layouts  17 us (2%)
  matrix products  11.5 us (2%)
    all_to_all x1, waiting for transfers between devices, body(): lax.all_to_all(jnp.stack([returned] * lax.axis_size('grp')), 'grp', 0, 0)  367 us
    ppermute x2, starting transfers between devices, extended(): lax.ppermute(tail, axis, [(i, (i + 1) % count) for i in range(ends)])  161 us
    all_to_all x1, blocking collectives, body(): lax.all_to_all(zlines, 'slab', split_axis=2, concat_axis=1, tiled=True)  70.3 us
    all_to_all x1, blocking collectives, body(): lax.all_to_all(seeded, 'slab', split_axis=1, concat_axis=2, tiled=True)  66.2 us
  transfers between devices with their start and end apart: 5, of which 4 were waited for; matrix products, arithmetic and copies ran while one was open for 0% of the time, Pallas kernels for 0%

profile of v1, /device:TPU:451, one launch (start us, length us, event | category | flops | bytes accessed | tf_op | source)
XLA Modules:
  0.0 748.1 jit_solution(1596121770959227905)
XLA Ops:
  0.0 0.8 add_select_fusion
  0.8 0.7 broadcast_select_fusion
  1.5 14.8 %scatter_custom_fusion = f32[65536]{0:T(1024)S(1)} fusion(s32[2048]{0:T(1024)S(1)} %add_select_fusion, f32[2048]{0:T(1024)S(1)} %broadcast_select_fusion, f32[]{:T(128)} %constant.45.clone.1), kind=kCustom, calls=%fused_computation.27 | custom fusion | flops 2048 | bytes 262148 | tf_op jit(solution)/shard_map/scatter-add | solution.py:47
  16.3 0.1 reshape.71
  16.4 1.5 copy.59
  18.0 0.1 fusion.4
  18.1 66.2 %all_to_all.23 = f32[5,64,4,256]{3,2,0,1:T(4,128)S(1)} all-to-all(f32[5,64,4,256]{3,2,0,1:T(4,128)S(1)} %fusion.4), channel_id=1, replica_groups=mesh['slab'=64,'grp'=8] {'slab'}, dimensions={1} | all-to-all | bytes 2621440 | tf_op jit(solution)/shard_map/all_to_all | solution.py:51
  84.3 0.2 copy.60
  84.5 0.5 reshape.72
  85.0 2.2 convolution_bitcast_fusion.1
  87.2 2.3 convolution_bitcast_fusion
  89.5 1.3 copy.63
  90.8 70.3 %all_to_all.24 = f32[5,1,256,256]{3,1,0,2:T(1,128)S(1)} all-to-all(f32[5,1,256,256]{3,1,0,2:T(1,128)S(1)} %copy.63), channel_id=1, replica_groups=mesh['slab'=64,'grp'=8] {'slab'}, dimensions={2} | all-to-all | bytes 2621440 | tf_op jit(solution)/shard_map/all_to_all | solution.py:54
  161.1 0.3 copy.78
  161.4 0.8 copy.65
  162.2 5.1 stack.5
  167.3 14.2 %all-to-all-start.2 = ((f32[8,5,64,4,256]{4,2,3,1,0:T(8,128)}), f32[8,5,64,4,256]{4,2,3,1,0:T(8,128)}, u32[]{:S(2)}, u32[]{:S(2)}) async-start(f32[8,5,64,4,256]{4,2,3,1,0:T(8,128)} %stack.5), calls=%async_computation.2 | async-start | bytes 20971520 | tf_op jit(solution)/shard_map/all_to_all | solution.py:59
  181.6 366.7 %all-to-all-done.2 = f32[8,5,64,4,256]{4,2,3,1,0:T(8,128)} async-done(((f32[8,5,64,4,256]{4,2,3,1,0:T(8,128)}), f32[8,5,64,4,256]{4,2,3,1,0:T(8,128)}, u32[]{:S(2)}, u32[]{:S(2)}) %all-to-all-start.2) | async-done | bytes 10485792 | tf_op jit(solution)/shard_map/all_to_all | solution.py:59
  548.4 4.9 copy.66
  553.2 7.0 fusion
  560.3 0.1 fusion.10
  560.3 157.6 %collective-permute-start = (f32[5,64,1,256]{3,1,2,0:T(8,128)S(1)}, f32[5,64,1,256]{3,1,2,0:T(8,128)S(1)}, u32[]{:S(2)}, u32[]{:S(2)}) collective-permute-start(f32[5,64,1,256]{3,1,2,0:T(8,128)S(1)} %get-tuple-element.19), channel_id=1, source_target_pairs={{0,8},{8,16},{16,24},{24,32},{32,40},{40,48},{48,56},{56,64},{64,7... | collective-permute-start | bytes 983048 | tf_op jit(solution)/shard_map/ppermute | solution.py:18
  717.9 1.9 collective-permute-start.1
  719.9 0.1 convert_element_type.12
  720.0 1.9 collective-permute-done
  721.9 4.7 collective-permute-done.1
  726.7 1.9 collective-permute-start.2
  728.6 3.5 collective-permute-start.3
  732.1 0.2 fusion.3
  732.5 11.7 %collective-permute-done.3 = f32[5,1,6,256]{3,1,2,0:T(1,128)S(1)} collective-permute-done((f32[5,1,6,256]{3,1,2,0:T(1,128)S(1)}, f32[5,1,6,256]{3,1,2,0:T(1,128)S(1)}, u32[]{:S(2)}, u32[]{:S(2)}) %collective-permute-start.3) | collective-permute-done | bytes 30752 | tf_op jit(solution)/shard_map/ppermute | solution.py:18
  744.2 2.0 multiply_add_fusion
  746.2 1.9 copy.72
  (20 shorter events, 0.4 us)
Async XLA Ops:
  0.0 84.9 %copy-start = (f32[256,256]{1,0:T(8,128)S(1)}, f32[256,256]{1,0:T(8,128)}, u32[]{:S(2)}) copy-start(f32[256,256]{1,0:T(8,128)} %param.23) | copy-start | bytes 786436
  84.9 2.2 copy-start.3
  167.3 14.2 %copy-start.2 = (s32[64,4,256]{2,1,0:T(4,128)S(1)}, s32[64,4,256]{2,1,0:T(4,128)}, u32[]{:S(2)}) copy-start(s32[64,4,256]{2,1,0:T(4,128)} %param.16) | copy-start | bytes 786436
  167.3 381.0 %all-to-all-start.2 = ((f32[8,5,64,4,256]{4,2,3,1,0:T(8,128)}), f32[8,5,64,4,256]{4,2,3,1,0:T(8,128)}, u32[]{:S(2)}, u32[]{:S(2)}) async-start(f32[8,5,64,4,256]{4,2,3,1,0:T(8,128)} %stack.5), calls=%async_computation.2 | async-start | bytes 20971520 | tf_op jit(solution)/shard_map/all_to_all | solution.py:59
  548.4 4.9 copy-start.4
  560.3 159.6 %copy-start.1 = (bf16[3,64,4,256]{3,2,1,0:T(4,128)(2,1)S(1)}, bf16[3,64,4,256]{3,2,1,0:T(4,128)(2,1)}, u32[]{:S(2)}) copy-start(bf16[3,64,4,256]{3,2,1,0:T(4,128)(2,1)} %param.14) | copy-start | bytes 1179652
  560.3 161.6 %collective-permute-start = (f32[5,64,1,256]{3,1,2,0:T(8,128)S(1)}, f32[5,64,1,256]{3,1,2,0:T(8,128)S(1)}, u32[]{:S(2)}, u32[]{:S(2)}) collective-permute-start(f32[5,64,1,256]{3,1,2,0:T(8,128)S(1)} %get-tuple-element.19), channel_id=1, source_target_pairs={{0,8},{8,16},{16,24},{24,32},{32,40},{40,48},{48,56},{56,64},{64,7... | collective-permute-start | bytes 983048 | tf_op jit(solution)/shard_map/ppermute | solution.py:18
  717.9 8.7 %collective-permute-start.1 = (f32[5,64,1,256]{3,1,2,0:T(8,128)S(1)}, f32[5,64,1,256]{3,1,2,0:T(8,128)S(1)}, u32[]{:S(2)}, u32[]{:S(2)}) collective-permute-start(f32[5,64,1,256]{3,1,2,0:T(8,128)S(1)} %get-tuple-element.20), channel_id=1, source_target_pairs={{8,0},{16,8},{24,16},{32,24},{40,32},{48,40},{56,48},{64,56},{72,6... | collective-permute-start | bytes 983048 | tf_op jit(solution)/shard_map/ppermute | solution.py:20
  726.7 5.9 collective-permute-start.2
  728.6 3.9 copy-start.5
  728.6 15.6 %collective-permute-start.3 = (f32[5,1,6,256]{3,1,2,0:T(1,128)S(1)}, f32[5,1,6,256]{3,1,2,0:T(1,128)S(1)}, u32[]{:S(2)}, u32[]{:S(2)}) collective-permute-start(f32[5,1,6,256]{3,1,2,0:T(1,128)S(1)} %get-tuple-element.17), channel_id=1, source_target_pairs={{0,1},{1,2},{2,3},{3,4},{4,5},{5,6},{6,7},{8,9},{9,10},{10,11},{11... | collective-permute-start | bytes 92168 | tf_op jit(solution)/shard_map/ppermute | solution.py:18
